TPU v7x, 128 devices: a whole 4x4x4 slice. The times are simulated.
128 devices in a mesh: leaf: 64 (over y_hi, x, z, core), rhs: 2 (over y_lo).
Axes of the slice: x: 4, y: 4 (y_hi: 2, y_lo: 2; y = y_hi * 2 + y_lo), z: 4, core: 2. Of those that a mesh axis runs over, the one named last changes fastest.
Arguments:
- rhs: bfloat16 [524288, 512], P('leaf', 'rhs'), may hold values from -6 to 6
- source_basis: bfloat16 [4096, 128, 128], P('leaf', None, 'rhs'), may hold values from -0.5 to 0.5
- target_basis: bfloat16 [4096, 128, 128], P('leaf', None, 'rhs'), may hold values from -0.5 to 0.5
- near_blocks: bfloat16 [4096, 2, 128, 128], P('leaf', None, None, 'rhs'), may hold values from -0.375 to 0.375
- near_offsets: int32 [4096, 2], P('leaf'), may hold values from -2 to 2
- source_values: bfloat16 [3, 2048, 2, 2, 128, 128], P(None, 'leaf', None, None, 'rhs'), may hold values from -0.375 to 0.375
- source_scales: float32 [3, 2048, 2, 2, 128], P(None, 'leaf'), may hold values from 0.2 to 2
- target_values: bfloat16 [3, 2048, 2, 2, 128, 128], P(None, 'leaf', None, None, 'rhs'), may hold values from -0.375 to 0.375
- target_scales: float32 [3, 2048, 2, 2, 128], P(None, 'leaf'), may hold values from 0.2 to 2
Outputs:
- product: bfloat16 [524288, 512], P('leaf', 'rhs')
All inputs are finite; a program needn't handle non-finite values.
Results may differ from a plain program's by a relative error of at most 0.01.
Values may be sent and summed in bfloat16 or wider, within the bound.
A program may use at most 192 MiB of HBM per device.

v0:
```python
import jax
import jax.numpy as jnp
from jax import lax
from jax.sharding import PartitionSpec as P

REACH = 2
SRC_LEVELS = 3
TGT_LEVELS = 3


def padded_2(cells, sides, width):
    for axis, dim in sides:
        count = lax.axis_size(axis)
        ends = count - 1
        head = lax.slice_in_dim(cells, 0, width, axis=dim)
        tail = lax.slice_in_dim(cells, cells.shape[dim] - width, cells.shape[dim], axis=dim)
        cells = jnp.concatenate(
            [
                lax.ppermute(tail, axis, [(i, (i + 1) % count) for i in range(ends)]),
                cells,
                lax.ppermute(head, axis, [((i + 1) % count, i) for i in range(ends)]),
            ],
            axis=dim,
        )
    return cells


def dequantize(values, scales):
    return (values.astype(jnp.float32) * scales[..., None, :]).astype(jnp.bfloat16)


def butterfly_level(coefficients, blocks, bit_index):
    box_total, columns, rank = coefficients.shape
    outputs = blocks.shape[-2]
    low_span = 2**bit_index
    high_span = box_total // (2 * low_span)
    inputs = coefficients.reshape(high_span, 2, low_span, columns, rank)
    matrices = blocks.reshape(high_span, low_span, 2, 2, outputs, rank)
    mixed = jnp.einsum("hclnr,hlocsr->holns", inputs, matrices, preferred_element_type=jnp.float32)
    return mixed.reshape(box_total, columns, outputs).astype(jnp.bfloat16)


def apply_level(coefficients, scales, bit_index, gathered):
    return butterfly_level(coefficients, dequantize(gathered, scales), bit_index)


def on_device(
    rhs,
    source_basis,
    target_basis,
    near_blocks,
    near_offsets,
    source_values,
    source_scales,
    target_values,
    target_scales,
):
    box_count = source_basis.shape[0]
    box_rows = source_basis.shape[1]
    columns = rhs.shape[1]
    rhs_boxes = rhs.reshape(box_count, box_rows, columns)
    basis_in, basis_out, near_full = (
        lax.all_gather(source_basis, "rhs", axis=2, tiled=True),
        lax.all_gather(target_basis, "rhs", axis=2, tiled=True),
        lax.all_gather(near_blocks, "rhs", axis=3, tiled=True),
    )
    source_tables, target_tables = (
        lax.all_gather(source_values, "rhs", axis=4, tiled=True),
        lax.all_gather(target_values, "rhs", axis=4, tiled=True),
    )
    coefficients = jnp.einsum(
        "bmc,bmr->bcr", rhs_boxes, basis_in, preferred_element_type=jnp.float32
    ).astype(jnp.bfloat16)
    for level_index in range(SRC_LEVELS):
        coefficients = apply_level(
            coefficients, source_scales[level_index], level_index, source_tables[level_index]
        )
    padded = padded_2(rhs_boxes, (("leaf", 0),), REACH)
    source_index = jnp.arange(box_count, dtype=jnp.int32)[:, None] + REACH + near_offsets
    selected = jnp.take(padded, source_index, axis=0)
    near_field = jnp.einsum(
        "bkmn,bknc->bmc", near_full, selected, preferred_element_type=jnp.float32
    )
    row_coefficients = lax.all_to_all(coefficients, "leaf", split_axis=0, concat_axis=0, tiled=True)
    for level_index in range(TGT_LEVELS):
        row_coefficients = apply_level(
            row_coefficients, target_scales[level_index], level_index, target_tables[level_index]
        )
    far_field = jnp.einsum(
        "bmr,bcr->bmc", basis_out, row_coefficients, preferred_element_type=jnp.float32
    )
    return (far_field + near_field).astype(jnp.bfloat16).reshape(box_count * box_rows, columns)


def solution(mesh):
    placed = (
        P("leaf", "rhs"),
        P("leaf", None, "rhs"),
        P("leaf", None, "rhs"),
        P("leaf", None, None, "rhs"),
        P("leaf", None),
        P(None, "leaf", None, None, "rhs", None),
        P(None, "leaf", None, None, None),
        P(None, "leaf", None, None, "rhs", None),
        P(None, "leaf", None, None, None),
    )
    return jax.shard_map(
        on_device, mesh=mesh, in_specs=placed, out_specs=P("leaf", "rhs"), check_vma=False
    )
```

profile of v0, /device:TPU:1, one launch (start us, length us, event | category | flops | bytes accessed | tf_op | source)
XLA Modules:
  0.0 526.6 jit_solution(11540010097013420315)
XLA Ops:
  6.5 0.0 all-gather.10.cloned.1.call-start
  6.5 0.7 all-gather.10.cloned.1.call-update
  7.3 0.0 all-gather.8.cloned.1.call-start
  7.3 0.7 all-gather.8.cloned.1.call-update
  8.0 0.0 copy-start.2
  8.0 0.0 all-gather.6.cloned.1.call-start
  8.1 0.7 all-gather.6.cloned.1.call-update
  8.8 0.2 copy-done.2
  9.0 38.7 %all-gather.10.cloned.1.call-done = bf16[64,128,128]{1,2,0:T(8,128)(2,1)} async-done(((bf16[64,128,64]{1,2,0:T(8,128)(2,1)}), bf16[64,128,128]{1,2,0:T(8,128)(2,1)}) %all-gather.10.cloned.1.call-update) | async-done | bytes 2097168 | tf_op jit(solution)/shard_map/all_gather | solution.py:63
  47.7 6.2 %convolution_convert_fusion = bf16[64,256,128]{2,1,0:T(8,128)(2,1)} fusion(bf16[64,128,256]{2,1,0:T(8,128)(2,1)} %bitcast.118, bf16[64,128,128]{1,2,0:T(8,128)(2,1)} %all-gather.10.cloned.1.call-done), kind=kOutput, calls=%fused_computation.48 | convolution fusion | flops 538968064 | bytes 10485760 | tf_op jit(solution)/shard_map/bmc,bmr->bcr/dot_general | solution.py:71
  53.9 151.5 %all-gather.8.cloned.1.call-done = bf16[3,32,2,2,128,128]{5,4,3,2,1,0:T(8,128)(2,1)} async-done(((bf16[3,32,2,2,64,128]{5,4,3,2,1,0:T(8,128)(2,1)}), bf16[3,32,2,2,128,128]{5,4,3,2,1,0:T(8,128)(2,1)}) %all-gather.8.cloned.1.call-update) | async-done | bytes 12582928 | tf_op jit(solution)/shard_map/all_gather | solution.py:68
  205.4 5.4 %fusion.61 = (bf16[1,32,2,2,128,128]{5,4,3,2,1,0:T(8,128)(2,1)}, bf16[1,32,2,2,128,128]{5,4,3,2,1,0:T(8,128)(2,1)S(1)}) fusion(bf16[3,32,2,2,128,128]{5,4,3,2,1,0:T(8,128)(2,1)} %all-gather.8.cloned.1.call-done), kind=kLoop, calls=%fused_computation.57 | loop fusion | bytes 16777216 | tf_op jit(solution)/shard_map/slice | solution.py:76
  210.8 0.8 copy-done
  211.5 3.5 bitcast_convert_fusion.5
  215.0 3.6 fusion.10
  218.6 6.9 %copy.17 = bf16[16,2,2,256,128]{4,3,2,1,0:T(8,128)(2,1)} copy(bf16[16,2,2,256,128]{3,4,1,2,0:T(8,128)(2,1)} %fusion.10) | data formatting | bytes 8388608 | tf_op jit(solution)/shard_map/convert_element_type | solution.py:40
  225.6 7.4 %fusion.11 = bf16[8,2,4,256,128]{3,4,1,2,0:T(8,128)(2,1)} fusion(bf16[8,2,4,256,128,1]{4,3,2,1,0,5:T(8,128)(2,1)} %bitcast.123, bf16[8,4,2,2,128,128]{5,4,3,2,1,0:T(8,128)(2,1)} %bitcast.126, f32[8,4,2,2,128]{4,3,2,1,0:T(2,128)S(1)} %bitcast.133), kind=kOutput, calls=%fused_computation.26 | convolution fusion | flops 1082130432 | bytes 12648448 | tf_op jit(solution)/shard_map/hclnr,hlocsr->holns/dot_general | solution.py:39
  233.0 6.5 %copy.19 = bf16[8,2,4,256,128]{4,3,2,1,0:T(8,128)(2,1)} copy(bf16[8,2,4,256,128]{3,4,1,2,0:T(8,128)(2,1)} %fusion.11) | data formatting | bytes 8388608 | tf_op jit(solution)/shard_map/convert_element_type | solution.py:40
  239.5 10.7 %all-to-all-start = ((bf16[64,256,128]{2,1,0:T(8,128)(2,1)}), bf16[64,256,128]{2,1,0:T(8,128)(2,1)}, u32[]{:S(2)}, u32[]{:S(2)}) async-start(bf16[64,256,128]{2,1,0:T(8,128)(2,1)} %bitcast.121), calls=%async_computation | async-start | bytes 8388608 | tf_op jit(solution)/shard_map/all_to_all | solution.py:84
  250.3 0.0 all-gather.12.cloned.1.call-start
  250.3 0.5 all-gather.12.cloned.1.call-update
  250.8 0.0 all-gather.14.cloned.1.call-start
  250.9 0.5 all-gather.14.cloned.1.call-update
  251.4 1.0 fusion.62
  252.4 3.5 collective-permute-start
  256.0 2.1 collective-permute-start.1
  258.1 0.0 copy-done.3
  258.1 0.0 copy-done.4
  258.1 0.1 copy.25
  258.2 0.1 reshape.106
  258.4 0.1 copy.24
  258.5 13.0 %collective-permute-done = bf16[2,128,256]{2,1,0:T(8,128)(2,1)S(1)} collective-permute-done((bf16[2,128,256]{2,1,0:T(8,128)(2,1)S(1)}, bf16[2,128,256]{2,1,0:T(8,128)(2,1)S(1)}, u32[]{:S(2)}, u32[]{:S(2)}) %collective-permute-start) | collective-permute-done | bytes 131104 | tf_op jit(solution)/shard_map/ppermute | solution.py:19
  271.5 2.2 collective-permute-done.1
  273.7 4.0 pad_maximum_fusion
  277.7 8.8 %gather_fusion = bf16[128,128,256]{2,1,0:T(8,128)(2,1)} fusion(bf16[68,128,256]{2,1,0:T(8,128)(2,1)} %pad_maximum_fusion, s32[1024]{0:T(1024)S(1)} %pad_clamp_fusion), kind=kCustom, calls=%fused_computation | custom fusion | bytes 16777728 | tf_op jit(solution)/shard_map/jit(_take)/gather | solution.py:80
  286.5 121.5 %all-gather.6.cloned.1.call-done = bf16[3,32,2,2,128,128]{5,4,3,2,1,0:T(8,128)(2,1)} async-done(((bf16[3,32,2,2,64,128]{5,4,3,2,1,0:T(8,128)(2,1)}), bf16[3,32,2,2,128,128]{5,4,3,2,1,0:T(8,128)(2,1)}) %all-gather.6.cloned.1.call-update) | async-done | bytes 12582928 | tf_op jit(solution)/shard_map/all_gather | solution.py:69
  408.0 6.2 %fusion.60 = (bf16[1,32,2,2,128,128]{5,4,3,2,1,0:T(8,128)(2,1)}, bf16[1,32,2,2,128,128]{5,4,3,2,1,0:T(8,128)(2,1)}) fusion(bf16[3,32,2,2,128,128]{5,4,3,2,1,0:T(8,128)(2,1)} %all-gather.6.cloned.1.call-done), kind=kLoop, calls=%fused_computation.56 | loop fusion | bytes 16777216 | tf_op jit(solution)/shard_map/slice | solution.py:87
  414.2 0.0 all-to-all-done
  414.2 4.9 bitcast_convert_fusion.2
  419.1 0.0 copy-done.1
  419.1 3.2 fusion.12
  422.4 6.6 %copy.21 = bf16[16,2,2,256,128]{4,3,2,1,0:T(8,128)(2,1)} copy(bf16[16,2,2,256,128]{3,4,1,2,0:T(8,128)(2,1)} %fusion.12) | data formatting | bytes 8388608 | tf_op jit(solution)/shard_map/convert_element_type | solution.py:40
  429.0 6.7 %fusion.13 = bf16[8,2,4,256,128]{3,4,1,2,0:T(8,128)(2,1)} fusion(bf16[8,2,4,256,128,1]{4,3,2,1,0,5:T(8,128)(2,1)} %bitcast.124, bf16[8,4,2,2,128,128]{5,4,3,2,1,0:T(8,128)(2,1)} %bitcast.125, f32[8,4,2,2,128]{4,3,2,1,0:T(2,128)S(1)} %bitcast.131), kind=kOutput, calls=%fused_computation.28 | convolution fusion | flops 1082130432 | bytes 12648448 | tf_op jit(solution)/shard_map/hclnr,hlocsr->holns/dot_general | solution.py:39
  435.7 6.4 %copy.23 = bf16[8,2,4,256,128]{4,3,2,1,0:T(8,128)(2,1)} copy(bf16[8,2,4,256,128]{3,4,1,2,0:T(8,128)(2,1)} %fusion.13) | data formatting | bytes 8388608 | tf_op jit(solution)/shard_map/convert_element_type | solution.py:40
  442.1 6.1 %all-gather.12.cloned.1.call-done = bf16[64,128,128]{1,2,0:T(8,128)(2,1)} async-done(((bf16[64,128,64]{1,2,0:T(8,128)(2,1)}), bf16[64,128,128]{1,2,0:T(8,128)(2,1)}) %all-gather.12.cloned.1.call-update) | async-done | bytes 2097168 | tf_op jit(solution)/shard_map/all_gather | solution.py:64
  448.3 7.4 %fusion.65 = f32[64,256,128]{1,2,0:T(8,128)} fusion(bf16[64,256,128]{2,1,0:T(8,128)(2,1)} %bitcast.120, bf16[64,128,128]{1,2,0:T(8,128)(2,1)} %all-gather.12.cloned.1.call-done), kind=kOutput, calls=%fused_computation.61 | convolution fusion | flops 536870912 | bytes 14680064 | tf_op jit(solution)/shard_map/bmr,bcr->bmc/dot_general | solution.py:89
  455.7 54.3 %all-gather.14.cloned.1.call-done = bf16[64,2,128,128]{2,3,1,0:T(8,128)(2,1)} async-done(((bf16[64,2,128,64]{2,3,1,0:T(8,128)(2,1)}), bf16[64,2,128,128]{2,3,1,0:T(8,128)(2,1)}) %all-gather.14.cloned.1.call-update) | async-done | bytes 4194320 | tf_op jit(solution)/shard_map/all_gather | solution.py:65
  510.0 10.1 %fusion.6 = bf16[64,256,128]{1,2,0:T(8,128)(2,1)} fusion(f32[64,256,128]{1,2,0:T(8,128)} %fusion.65, bf16[64,2,128,128]{2,3,1,0:T(8,128)(2,1)} %all-gather.14.cloned.1.call-done, bf16[64,2,128,256]{3,2,1,0:T(8,128)(2,1)} %bitcast.117, pred[64,2]{1,0:T(8,128)(4,1)S(1)} %copy.24), kind=kOutput, calls=%fused_computation.14 | convolution fusion | flops 1082130432 | bytes 25165952 | tf_op jit(solution)/shard_map/bkmn,bknc->bmc/dot_general | solution.py:81
  (9 shorter events, 0.1 us)
Async XLA Ops:
  6.5 41.1 %all-gather.10.cloned.1.call-start = ((), (), s32[]{:S(2)}) async-start(), calls=%async_computation.3 | async-start | bytes 3145728 | tf_op jit(solution)/shard_map/all_gather | solution.py:63
  7.3 198.1 %all-gather.8.cloned.1.call-start = ((), (), s32[]{:S(2)}) async-start(), calls=%async_computation.2 | async-start | bytes 18874368 | tf_op jit(solution)/shard_map/all_gather | solution.py:68
  8.0 0.9 copy-start.2
  8.0 400.0 %all-gather.6.cloned.1.call-start = ((), (), s32[]{:S(2)}) async-start(), calls=%async_computation.1 | async-start | bytes 18874368 | tf_op jit(solution)/shard_map/all_gather | solution.py:69
  205.4 6.2 %copy-start = (bf16[64,256,128]{2,1,0:T(8,128)(2,1)S(1)}, bf16[64,256,128]{2,1,0:T(8,128)(2,1)}, u32[]{:S(2)}) copy-start(bf16[64,256,128]{2,1,0:T(8,128)(2,1)} %convolution_convert_fusion) | copy-start | bytes 12582916
  239.5 18.6 %copy-start.3 = (f32[3,32,2,2,128]{4,3,2,1,0:T(2,128)S(1)}, f32[3,32,2,2,128]{4,3,2,1,0:T(2,128)}, u32[]{:S(2)}) copy-start(f32[3,32,2,2,128]{4,3,2,1,0:T(2,128)} %param.17) | copy-start | bytes 589828
  239.5 18.6 %copy-start.4 = (s32[64,2]{0,1:T(2,128)S(1)}, s32[64,2]{0,1:T(2,128)}, u32[]{:S(2)}) copy-start(s32[64,2]{0,1:T(2,128)} %param.13) | copy-start | bytes 1540
  239.5 174.7 %all-to-all-start = ((bf16[64,256,128]{2,1,0:T(8,128)(2,1)}), bf16[64,256,128]{2,1,0:T(8,128)(2,1)}, u32[]{:S(2)}, u32[]{:S(2)}) async-start(bf16[64,256,128]{2,1,0:T(8,128)(2,1)} %bitcast.121), calls=%async_computation | async-start | bytes 8388608 | tf_op jit(solution)/shard_map/all_to_all | solution.py:84
  250.3 198.0 %all-gather.12.cloned.1.call-start = ((), (), s32[]{:S(2)}) async-start(), calls=%async_computation.4 | async-start | bytes 3145728 | tf_op jit(solution)/shard_map/all_gather | solution.py:64
  250.8 259.2 %all-gather.14.cloned.1.call-start = ((), (), s32[]{:S(2)}) async-start(), calls=%async_computation.5 | async-start | bytes 6291456 | tf_op jit(solution)/shard_map/all_gather | solution.py:65
  252.4 19.1 %collective-permute-start = (bf16[2,128,256]{2,1,0:T(8,128)(2,1)S(1)}, bf16[2,128,256]{2,1,0:T(8,128)(2,1)S(1)}, u32[]{:S(2)}, u32[]{:S(2)}) collective-permute-start(bf16[2,128,256]{2,1,0:T(8,128)(2,1)S(1)} %bitcast.130), channel_id=1, source_target_pairs={{0,2},{2,4},{4,6},{6,8},{8,10},{10,12},{12,14},{14,16},{16,18},{18... | collective-permute-start | bytes 393224 | tf_op jit(solution)/shard_map/ppermute | solution.py:19
  256.0 17.8 %collective-permute-start.1 = (bf16[2,128,256]{2,1,0:T(8,128)(2,1)S(1)}, bf16[2,128,256]{2,1,0:T(8,128)(2,1)S(1)}, u32[]{:S(2)}, u32[]{:S(2)}) collective-permute-start(bf16[2,128,256]{2,1,0:T(8,128)(2,1)S(1)} %bitcast.129), channel_id=1, source_target_pairs={{2,0},{4,2},{6,4},{8,6},{10,8},{12,10},{14,12},{16,14},{18,16},{20... | collective-permute-start | bytes 393224 | tf_op jit(solution)/shard_map/ppermute | solution.py:21
  414.2 4.9 copy-start.1
Sparse Core Ops, SparseCore 0:
  9.0 38.6 all-gather.9
  49.3 155.9 all-gather.7
  207.0 200.9 all-gather.5
  409.5 38.7 all-gather.11
  449.8 60.2 all-gather.13
where the time goes:
time: 528 us; the launch traced here: 527 us
  waiting for transfers between devices  391 us (74%)
  matrix products  53.1 us (10%)
  local copies, waits for them, and re-layouts  49.3 us (9%)
  starting transfers between devices  16.5 us (3%)
  between operations  13.3 us (3%)
    all_gather x1, waiting for transfers between devices, on_device(): lax.all_gather(source_values, 'rhs', axis=4, tiled=True)  152 us
    all_gather x1, waiting for transfers between devices, on_device(): lax.all_gather(target_values, 'rhs', axis=4, tiled=True)  121 us
    all_gather x1, waiting for transfers between devices, on_device(): lax.all_gather(near_blocks, 'rhs', axis=3, tiled=True)  54.3 us
    all_gather x1, waiting for transfers between devices, on_device(): lax.all_gather(source_basis, 'rhs', axis=2, tiled=True)  38.7 us
    dot_general x6, matrix products, butterfly_level(): jnp.einsum('hclnr,hlocsr->holns', inputs, matrices, preferred_element_typ...  29.3 us
    convert_element_type x4, local copies, waits for them, and re-layouts, butterfly_level(): return mixed.reshape(box_total, columns, outputs).astype(jnp.bfloat16)  26.5 us
    ppermute x1, waiting for transfers between devices, padded_2(): lax.ppermute(tail, axis, [(i, (i + 1) % count) for i in range(ends)])  13 us
    all_to_all x1, starting transfers between devices, on_device(): lax.all_to_all(coefficients, 'leaf', split_axis=0, concat_axis=0, tiled=T...  10.7 us
  transfers between devices with their start and end apart: 8, of which 7 were waited for; matrix products, arithmetic and copies ran while one was open for 18% of the time, Pallas kernels for 0%

commit v1 on v0

--- a/solution.py
+++ b/solution.py
@@ -6,6 +6,11 @@
 REACH = 2
 SRC_LEVELS = 3
 TGT_LEVELS = 3
+
+
+def gather_blocks(block, axis, dim):
+    blocks = lax.all_gather(block, axis)
+    return jnp.concatenate(blocks, axis=dim)
 
 
 def padded_2(cells, sides, width):
@@ -60,7 +65,7 @@
     columns = rhs.shape[1]
     rhs_boxes = rhs.reshape(box_count, box_rows, columns)
     basis_in, basis_out, near_full = (
-        lax.all_gather(source_basis, "rhs", axis=2, tiled=True),
+        gather_blocks(source_basis, "rhs", 2),
         lax.all_gather(target_basis, "rhs", axis=2, tiled=True),
         lax.all_gather(near_blocks, "rhs", axis=3, tiled=True),
     )

time: 528 us -> 528 us (level)
  no operation moved by 1% of the time
where the time goes in v1:
time: 528 us; the launch traced here: 527 us
  waiting for transfers between devices  390 us (74%)
  local copies, waits for them, and re-layouts  52.1 us (10%)
  matrix products  50.2 us (10%)
  starting transfers between devices  16.5 us (3%)
  between operations  13.3 us (3%)
    all_gather x1, waiting for transfers between devices, on_device(): lax.all_gather(source_values, 'rhs', axis=4, tiled=True)  152 us
    all_gather x1, waiting for transfers between devices, on_device(): lax.all_gather(target_values, 'rhs', axis=4, tiled=True)  121 us
    all_gather x1, waiting for transfers between devices, on_device(): lax.all_gather(near_blocks, 'rhs', axis=3, tiled=True)  54.3 us
    all_gather x1, waiting for transfers between devices, gather_blocks(): blocks = lax.all_gather(block, axis)  38.7 us
    dot_general x6, matrix products, butterfly_level(): jnp.einsum('hclnr,hlocsr->holns', inputs, matrices, preferred_element_typ...  29.3 us
    convert_element_type x4, local copies, waits for them, and re-layouts, butterfly_level(): return mixed.reshape(box_total, columns, outputs).astype(jnp.bfloat16)  26.6 us
    ppermute x1, waiting for transfers between devices, padded_2(): lax.ppermute(tail, axis, [(i, (i + 1) % count) for i in range(ends)])  13 us
    all_to_all x1, starting transfers between devices, on_device(): lax.all_to_all(coefficients, 'leaf', split_axis=0, concat_axis=0, tiled=T...  10.7 us
  transfers between devices with their start and end apart: 8, of which 7 were waited for; matrix products, arithmetic and copies ran while one was open for 18% of the time, Pallas kernels for 0%

profile of v1, /device:TPU:1, one launch (start us, length us, event | category | flops | bytes accessed | tf_op | source)
XLA Modules:
  0.0 526.6 jit_solution(7762502982556161275)
XLA Ops:
  6.5 0.0 all-gather.15.cloned.1.call-start
  6.5 0.7 all-gather.15.cloned.1.call-update
  7.3 0.0 all-gather.9.cloned.1.call-start
  7.3 0.7 all-gather.9.cloned.1.call-update
  8.0 0.0 copy-start.3
  8.0 0.0 all-gather.7.cloned.1.call-start
  8.1 0.7 all-gather.7.cloned.1.call-update
  8.8 0.2 copy-done.3
  9.0 38.7 %all-gather.15.cloned.1.call-done = bf16[128,128,64]{1,2,0:T(8,128)(2,1)} async-done(((bf16[64,128,64]{1,2,0:T(8,128)(2,1)}), bf16[128,128,64]{1,2,0:T(8,128)(2,1)}) %all-gather.15.cloned.1.call-update) | async-done | bytes 2097168 | tf_op jit(solution)/shard_map/all_gather | solution.py:12
  47.7 1.9 copy.41
  49.6 0.9 copy-done
  50.5 3.3 convolution_convert_fusion
  53.8 151.6 %all-gather.9.cloned.1.call-done = bf16[3,32,2,2,128,128]{5,4,3,2,1,0:T(8,128)(2,1)} async-done(((bf16[3,32,2,2,64,128]{5,4,3,2,1,0:T(8,128)(2,1)}), bf16[3,32,2,2,128,128]{5,4,3,2,1,0:T(8,128)(2,1)}) %all-gather.9.cloned.1.call-update) | async-done | bytes 12582928 | tf_op jit(solution)/shard_map/all_gather | solution.py:73
  205.4 5.4 %fusion.61 = (bf16[1,32,2,2,128,128]{5,4,3,2,1,0:T(8,128)(2,1)}, bf16[1,32,2,2,128,128]{5,4,3,2,1,0:T(8,128)(2,1)S(1)}) fusion(bf16[3,32,2,2,128,128]{5,4,3,2,1,0:T(8,128)(2,1)} %all-gather.9.cloned.1.call-done), kind=kLoop, calls=%fused_computation.57 | loop fusion | bytes 16777216 | tf_op jit(solution)/shard_map/slice | solution.py:81
  210.8 0.8 copy-done.1
  211.5 3.5 bitcast_convert_fusion.5
  215.0 3.6 fusion.10
  218.6 7.0 %copy.45 = bf16[16,2,2,256,128]{4,3,2,1,0:T(8,128)(2,1)} copy(bf16[16,2,2,256,128]{3,4,1,2,0:T(8,128)(2,1)} %fusion.10) | data formatting | bytes 8388608 | tf_op jit(solution)/shard_map/convert_element_type | solution.py:45
  225.6 7.4 %fusion.11 = bf16[8,2,4,256,128]{3,4,1,2,0:T(8,128)(2,1)} fusion(bf16[8,2,4,256,128,1]{4,3,2,1,0,5:T(8,128)(2,1)} %bitcast.128, bf16[8,4,2,2,128,128]{5,4,3,2,1,0:T(8,128)(2,1)} %bitcast.131, f32[8,4,2,2,128]{4,3,2,1,0:T(2,128)S(1)} %bitcast.139), kind=kOutput, calls=%fused_computation.26 | convolution fusion | flops 1082130432 | bytes 12648448 | tf_op jit(solution)/shard_map/hclnr,hlocsr->holns/dot_general | solution.py:44
  233.0 6.6 %copy.47 = bf16[8,2,4,256,128]{4,3,2,1,0:T(8,128)(2,1)} copy(bf16[8,2,4,256,128]{3,4,1,2,0:T(8,128)(2,1)} %fusion.11) | data formatting | bytes 8388608 | tf_op jit(solution)/shard_map/convert_element_type | solution.py:45
  239.6 10.7 %all-to-all-start = ((bf16[64,256,128]{2,1,0:T(8,128)(2,1)}), bf16[64,256,128]{2,1,0:T(8,128)(2,1)}, u32[]{:S(2)}, u32[]{:S(2)}) async-start(bf16[64,256,128]{2,1,0:T(8,128)(2,1)} %bitcast.125), calls=%async_computation | async-start | bytes 8388608 | tf_op jit(solution)/shard_map/all_to_all | solution.py:89
  250.3 0.0 all-gather.11.cloned.1.call-start
  250.3 0.5 all-gather.11.cloned.1.call-update
  250.9 0.0 all-gather.13.cloned.1.call-start
  250.9 0.5 all-gather.13.cloned.1.call-update
  251.5 1.0 fusion.62
  252.5 3.5 collective-permute-start
  256.0 2.1 collective-permute-start.1
  258.2 0.1 copy.53
  258.3 0.1 reshape.114
  258.4 0.1 copy.52
  258.5 13.0 %collective-permute-done = bf16[2,128,256]{2,1,0:T(8,128)(2,1)S(1)} collective-permute-done((bf16[2,128,256]{2,1,0:T(8,128)(2,1)S(1)}, bf16[2,128,256]{2,1,0:T(8,128)(2,1)S(1)}, u32[]{:S(2)}, u32[]{:S(2)}) %collective-permute-start) | collective-permute-done | bytes 131104 | tf_op jit(solution)/shard_map/ppermute | solution.py:24
  271.6 2.2 collective-permute-done.1
  273.8 4.1 pad_maximum_fusion
  277.9 8.8 %gather_fusion = bf16[128,128,256]{2,1,0:T(8,128)(2,1)} fusion(bf16[68,128,256]{2,1,0:T(8,128)(2,1)} %pad_maximum_fusion, s32[1024]{0:T(1024)S(1)} %pad_clamp_fusion), kind=kCustom, calls=%fused_computation | custom fusion | bytes 16777728 | tf_op jit(solution)/shard_map/jit(_take)/gather | solution.py:85
  286.7 121.3 %all-gather.7.cloned.1.call-done = bf16[3,32,2,2,128,128]{5,4,3,2,1,0:T(8,128)(2,1)} async-done(((bf16[3,32,2,2,64,128]{5,4,3,2,1,0:T(8,128)(2,1)}), bf16[3,32,2,2,128,128]{5,4,3,2,1,0:T(8,128)(2,1)}) %all-gather.7.cloned.1.call-update) | async-done | bytes 12582928 | tf_op jit(solution)/shard_map/all_gather | solution.py:74
  408.0 6.2 %fusion.60 = (bf16[1,32,2,2,128,128]{5,4,3,2,1,0:T(8,128)(2,1)}, bf16[1,32,2,2,128,128]{5,4,3,2,1,0:T(8,128)(2,1)}) fusion(bf16[3,32,2,2,128,128]{5,4,3,2,1,0:T(8,128)(2,1)} %all-gather.7.cloned.1.call-done), kind=kLoop, calls=%fused_computation.56 | loop fusion | bytes 16777216 | tf_op jit(solution)/shard_map/slice | solution.py:92
  414.2 0.0 all-to-all-done
  414.2 4.9 bitcast_convert_fusion.2
  419.1 0.0 copy-done.2
  419.1 3.2 fusion.12
  422.4 6.6 %copy.49 = bf16[16,2,2,256,128]{4,3,2,1,0:T(8,128)(2,1)} copy(bf16[16,2,2,256,128]{3,4,1,2,0:T(8,128)(2,1)} %fusion.12) | data formatting | bytes 8388608 | tf_op jit(solution)/shard_map/convert_element_type | solution.py:45
  429.0 6.7 %fusion.13 = bf16[8,2,4,256,128]{3,4,1,2,0:T(8,128)(2,1)} fusion(bf16[8,2,4,256,128,1]{4,3,2,1,0,5:T(8,128)(2,1)} %bitcast.129, bf16[8,4,2,2,128,128]{5,4,3,2,1,0:T(8,128)(2,1)} %bitcast.130, f32[8,4,2,2,128]{4,3,2,1,0:T(2,128)S(1)} %bitcast.137), kind=kOutput, calls=%fused_computation.28 | convolution fusion | flops 1082130432 | bytes 12648448 | tf_op jit(solution)/shard_map/hclnr,hlocsr->holns/dot_general | solution.py:44
  435.7 6.4 %copy.51 = bf16[8,2,4,256,128]{4,3,2,1,0:T(8,128)(2,1)} copy(bf16[8,2,4,256,128]{3,4,1,2,0:T(8,128)(2,1)} %fusion.13) | data formatting | bytes 8388608 | tf_op jit(solution)/shard_map/convert_element_type | solution.py:45
  442.1 6.1 %all-gather.11.cloned.1.call-done = bf16[64,128,128]{1,2,0:T(8,128)(2,1)} async-done(((bf16[64,128,64]{1,2,0:T(8,128)(2,1)}), bf16[64,128,128]{1,2,0:T(8,128)(2,1)}) %all-gather.11.cloned.1.call-update) | async-done | bytes 2097168 | tf_op jit(solution)/shard_map/all_gather | solution.py:69
  448.3 7.4 %fusion.65 = f32[64,256,128]{1,2,0:T(8,128)} fusion(bf16[64,256,128]{2,1,0:T(8,128)(2,1)} %bitcast.124, bf16[64,128,128]{1,2,0:T(8,128)(2,1)} %all-gather.11.cloned.1.call-done), kind=kOutput, calls=%fused_computation.61 | convolution fusion | flops 536870912 | bytes 14680064 | tf_op jit(solution)/shard_map/bmr,bcr->bmc/dot_general | solution.py:94
  455.7 54.3 %all-gather.13.cloned.1.call-done = bf16[64,2,128,128]{2,3,1,0:T(8,128)(2,1)} async-done(((bf16[64,2,128,64]{2,3,1,0:T(8,128)(2,1)}), bf16[64,2,128,128]{2,3,1,0:T(8,128)(2,1)}) %all-gather.13.cloned.1.call-update) | async-done | bytes 4194320 | tf_op jit(solution)/shard_map/all_gather | solution.py:70
  510.0 10.1 %fusion.6 = bf16[64,256,128]{1,2,0:T(8,128)(2,1)} fusion(f32[64,256,128]{1,2,0:T(8,128)} %fusion.65, bf16[64,2,128,128]{2,3,1,0:T(8,128)(2,1)} %all-gather.13.cloned.1.call-done, bf16[64,2,128,256]{3,2,1,0:T(8,128)(2,1)} %bitcast.121, pred[64,2]{1,0:T(8,128)(4,1)S(1)} %copy.52), kind=kOutput, calls=%fused_computation.14 | convolution fusion | flops 1082130432 | bytes 25165952 | tf_op jit(solution)/shard_map/bkmn,bknc->bmc/dot_general | solution.py:86
  (12 shorter events, 0.1 us)
Async XLA Ops:
  6.5 41.1 %all-gather.15.cloned.1.call-start = ((), (), s32[]{:S(2)}) async-start(), calls=%async_computation.5 | async-start | bytes 3145728 | tf_op jit(solution)/shard_map/all_gather | solution.py:12
  7.3 198.1 %all-gather.9.cloned.1.call-start = ((), (), s32[]{:S(2)}) async-start(), calls=%async_computation.2 | async-start | bytes 18874368 | tf_op jit(solution)/shard_map/all_gather | solution.py:73
  8.0 0.9 copy-start.3
  8.0 400.0 %all-gather.7.cloned.1.call-start = ((), (), s32[]{:S(2)}) async-start(), calls=%async_computation.1 | async-start | bytes 18874368 | tf_op jit(solution)/shard_map/all_gather | solution.py:74
  47.7 2.8 copy-start
  205.4 6.2 %copy-start.1 = (bf16[64,256,128]{2,1,0:T(8,128)(2,1)S(1)}, bf16[64,256,128]{2,1,0:T(8,128)(2,1)}, u32[]{:S(2)}) copy-start(bf16[64,256,128]{2,1,0:T(8,128)(2,1)} %convolution_convert_fusion) | copy-start | bytes 12582916
  239.6 18.6 %copy-start.4 = (f32[3,32,2,2,128]{4,3,2,1,0:T(2,128)S(1)}, f32[3,32,2,2,128]{4,3,2,1,0:T(2,128)}, u32[]{:S(2)}) copy-start(f32[3,32,2,2,128]{4,3,2,1,0:T(2,128)} %param.17) | copy-start | bytes 589828
  239.6 18.6 %copy-start.5 = (s32[64,2]{0,1:T(2,128)S(1)}, s32[64,2]{0,1:T(2,128)}, u32[]{:S(2)}) copy-start(s32[64,2]{0,1:T(2,128)} %param.13) | copy-start | bytes 1540
  239.6 174.6 %all-to-all-start = ((bf16[64,256,128]{2,1,0:T(8,128)(2,1)}), bf16[64,256,128]{2,1,0:T(8,128)(2,1)}, u32[]{:S(2)}, u32[]{:S(2)}) async-start(bf16[64,256,128]{2,1,0:T(8,128)(2,1)} %bitcast.125), calls=%async_computation | async-start | bytes 8388608 | tf_op jit(solution)/shard_map/all_to_all | solution.py:89
  250.3 198.0 %all-gather.11.cloned.1.call-start = ((), (), s32[]{:S(2)}) async-start(), calls=%async_computation.3 | async-start | bytes 3145728 | tf_op jit(solution)/shard_map/all_gather | solution.py:69
  250.9 259.1 %all-gather.13.cloned.1.call-start = ((), (), s32[]{:S(2)}) async-start(), calls=%async_computation.4 | async-start | bytes 6291456 | tf_op jit(solution)/shard_map/all_gather | solution.py:70
  252.5 19.1 %collective-permute-start = (bf16[2,128,256]{2,1,0:T(8,128)(2,1)S(1)}, bf16[2,128,256]{2,1,0:T(8,128)(2,1)S(1)}, u32[]{:S(2)}, u32[]{:S(2)}) collective-permute-start(bf16[2,128,256]{2,1,0:T(8,128)(2,1)S(1)} %bitcast.136), channel_id=1, source_target_pairs={{0,2},{2,4},{4,6},{6,8},{8,10},{10,12},{12,14},{14,16},{16,18},{18... | collective-permute-start | bytes 393224 | tf_op jit(solution)/shard_map/ppermute | solution.py:24
  256.0 17.8 %collective-permute-start.1 = (bf16[2,128,256]{2,1,0:T(8,128)(2,1)S(1)}, bf16[2,128,256]{2,1,0:T(8,128)(2,1)S(1)}, u32[]{:S(2)}, u32[]{:S(2)}) collective-permute-start(bf16[2,128,256]{2,1,0:T(8,128)(2,1)S(1)} %bitcast.135), channel_id=1, source_target_pairs={{2,0},{4,2},{6,4},{8,6},{10,8},{12,10},{14,12},{16,14},{18,16},{20... | collective-permute-start | bytes 393224 | tf_op jit(solution)/shard_map/ppermute | solution.py:26
  414.2 4.9 copy-start.2
Sparse Core Ops, SparseCore 0:
  9.0 38.6 all-gather.14
  49.3 155.9 all-gather.8
  207.0 200.9 all-gather.6
  409.5 38.7 all-gather.10
  449.8 60.2 all-gather.12
